TPU v7x, 1024 devices: a whole 8x8x8 slice. The times are simulated.
1024 devices in a mesh: dp: 4 (over z_lo), expert: 32 (over z_hi, x, core), tensor: 8 (over y).
Axes of the slice: x: 8, y: 8, z: 8 (z_hi: 2, z_lo: 4; z = z_hi * 4 + z_lo), core: 2. Of those that a mesh axis runs over, the one named last changes fastest.
Arguments:
- tokens: bfloat16 [16384, 2048], P(('dp', 'expert')), may hold values from -6 to 6
- cotangent: bfloat16 [16384, 2048], P(('dp', 'expert')), may hold values from -6 to 6
- scores: float32 [16384, 8], P(('dp', 'expert')), may hold values from 0.05 to 1
- routes: int32 [16384, 1], P(('dp', 'expert')), may hold values from 0 to 63; in each aligned block of 128 rows (0 to 127, 128 to 255, ...) at most 4 rows name the same one
- w_gate: bfloat16 [64, 2048, 768], P('expert', 'dp', 'tensor'), may hold values from -0.125 to 0.125
- w_up: bfloat16 [64, 2048, 768], P('expert', 'dp', 'tensor'), may hold values from -0.125 to 0.125
- w_down: bfloat16 [64, 768, 2048], P('expert', 'tensor', 'dp'), may hold values from -0.21875 to 0.21875
Outputs:
- output: bfloat16 [16384, 2048], P(('dp', 'expert'), 'tensor')
- grad_tokens: bfloat16 [16384, 2048], P(('dp', 'expert'), 'tensor')
- grad_gate: float32 [64, 2048, 768], P('expert', 'dp', 'tensor')
- grad_up: float32 [64, 2048, 768], P('expert', 'dp', 'tensor')
- grad_down: float32 [64, 768, 2048], P('expert', 'tensor', 'dp')
Inputs may be any that keep to these rules, and one draw needn't show every extreme that they name: `routes`: each row names 1 different experts. Among the rows of one token block no expert is named more than 4 times, and 4 is reached.
All inputs are finite; a program needn't handle non-finite values.
Results may differ from a plain program's by a relative error of at most 0.019.
Values may be sent and summed in bfloat16 or wider, within the bound.
A program may use at most 32 MiB of HBM per device.

v0:
```python
import jax
import jax.numpy as jnp
from jax import lax
from jax.sharding import PartitionSpec as P


def slot_onehot(route_block, expert_count, capacity):
    flat = route_block.reshape(-1)
    member = (flat[:, None] == jnp.arange(expert_count, dtype=jnp.int32)[None, :]).astype(jnp.int32)
    before = jnp.cumsum(member, axis=0) - member
    place = jnp.sum(before * member, axis=1)
    slot_ids = flat * capacity + place
    return slot_ids[:, None] == jnp.arange(expert_count * capacity, dtype=jnp.int32)[None, :]


def on_device(tokens, cotangent, scores, routes, w_gate, w_up, w_down):
    highest = lax.Precision.HIGHEST
    tok_count = tokens.shape[0]
    model_width = tokens.shape[1]
    flight_count = routes.shape[1]
    owners = lax.axis_size("expert")
    local_count = w_gate.shape[0]
    expert_count = local_count * owners
    capacity = min(tok_count, 2 * tok_count * flight_count // expert_count)
    slot_total = expert_count * capacity
    table = slot_onehot(routes, expert_count, capacity)
    picker = table.astype(jnp.bfloat16)
    mix = (scores / jnp.sum(scores, axis=1, keepdims=True))[:, :flight_count]
    rep_x = jnp.repeat(tokens, flight_count, axis=0)
    rep_d = (mix[:, :, None] * cotangent.astype(jnp.float32)[:, None, :]).astype(jnp.bfloat16)
    rep_d = rep_d.reshape(tok_count * flight_count, model_width)
    send_x = jnp.einsum("rs,rd->sd", picker, rep_x, preferred_element_type=jnp.float32).astype(
        jnp.bfloat16
    )
    send_d = jnp.einsum("rs,rd->sd", picker, rep_d, preferred_element_type=jnp.float32).astype(
        jnp.bfloat16
    )
    full_gate, full_up, full_down = (
        lax.all_gather(w_gate, "dp", axis=1, tiled=True),
        lax.all_gather(w_up, "dp", axis=1, tiled=True),
        lax.all_gather(w_down, "dp", axis=2, tiled=True),
    )
    got_x, got_d = (
        lax.all_to_all(send_x, "expert", split_axis=0, concat_axis=0, tiled=True),
        lax.all_to_all(send_d, "expert", split_axis=0, concat_axis=0, tiled=True),
    )
    rows_x = got_x.reshape(owners, local_count, capacity, model_width)
    rows_d = got_d.reshape(owners, local_count, capacity, model_width)
    gate_act = jnp.einsum("oecd,edf->oecf", rows_x, full_gate, preferred_element_type=jnp.float32)
    up_act = jnp.einsum("oecd,edf->oecf", rows_x, full_up, preferred_element_type=jnp.float32)
    sigma = jax.nn.sigmoid(gate_act)
    silu_act = gate_act * sigma
    hidden = (silu_act * up_act).astype(jnp.bfloat16)
    part_out = jnp.einsum("oecf,efd->oecd", hidden, full_down, preferred_element_type=jnp.float32)
    back_grad = jnp.einsum("oecd,efd->oecf", rows_d, full_down, preferred_element_type=jnp.float32)
    grad_act_gate = (back_grad * up_act * sigma * (1.0 + gate_act * (1.0 - sigma))).astype(
        jnp.bfloat16
    )
    grad_act_up = (back_grad * silu_act).astype(jnp.bfloat16)
    part_in = jnp.einsum(
        "oecf,edf->oecd", grad_act_gate, full_gate, preferred_element_type=jnp.float32
    )
    part_in = part_in + jnp.einsum(
        "oecf,edf->oecd", grad_act_up, full_up, preferred_element_type=jnp.float32
    )
    spread = table.reshape(tok_count, flight_count, slot_total).astype(jnp.float32)
    weighted = jnp.einsum("tks,tk->ts", spread, mix, precision=highest)
    plain = jnp.sum(spread, axis=1)
    summed_out, summed_in = (
        lax.psum_scatter(
            part_out.astype(jnp.bfloat16), "tensor", scatter_dimension=3, tiled=True
        ).astype(jnp.float32),
        lax.psum_scatter(
            part_in.astype(jnp.bfloat16), "tensor", scatter_dimension=3, tiled=True
        ).astype(jnp.float32),
    )
    back_out, back_in = (
        lax.all_to_all(
            summed_out.astype(jnp.bfloat16), "expert", split_axis=0, concat_axis=0, tiled=True
        ).astype(summed_out.dtype),
        lax.all_to_all(
            summed_in.astype(jnp.bfloat16), "expert", split_axis=0, concat_axis=0, tiled=True
        ).astype(summed_in.dtype),
    )
    flat_out = back_out.reshape(slot_total, back_out.shape[3])
    flat_in = back_in.reshape(slot_total, back_in.shape[3])
    output = jnp.dot(weighted, flat_out, precision=highest).astype(jnp.bfloat16)
    grad_tokens = jnp.dot(plain, flat_in, precision=highest).astype(jnp.bfloat16)
    term_gate = jnp.einsum(
        "oecd,oecf->edf", rows_x, grad_act_gate, preferred_element_type=jnp.float32
    )
    term_up = jnp.einsum("oecd,oecf->edf", rows_x, grad_act_up, preferred_element_type=jnp.float32)
    term_down = jnp.einsum("oecf,oecd->efd", hidden, rows_d, preferred_element_type=jnp.float32)
    grad_gate, grad_up, grad_down = (
        lax.psum_scatter(
            term_gate.astype(jnp.bfloat16), "dp", scatter_dimension=1, tiled=True
        ).astype(jnp.float32),
        lax.psum_scatter(
            term_up.astype(jnp.bfloat16), "dp", scatter_dimension=1, tiled=True
        ).astype(jnp.float32),
        lax.psum_scatter(
            term_down.astype(jnp.bfloat16), "dp", scatter_dimension=2, tiled=True
        ).astype(jnp.float32),
    )
    return (output, grad_tokens, grad_gate, grad_up, grad_down)


def solution(mesh):
    in_specs = (
        P(("dp", "expert"), None),
        P(("dp", "expert"), None),
        P(("dp", "expert"), None),
        P(("dp", "expert"), None),
        P("expert", "dp", "tensor"),
        P("expert", "dp", "tensor"),
        P("expert", "tensor", "dp"),
    )
    out_specs = (
        P(("dp", "expert"), "tensor"),
        P(("dp", "expert"), "tensor"),
        P("expert", "dp", "tensor"),
        P("expert", "dp", "tensor"),
        P("expert", "tensor", "dp"),
    )
    return jax.shard_map(
        on_device, mesh=mesh, in_specs=in_specs, out_specs=out_specs, check_vma=False
    )
```

profile of v0, /device:TPU:1, one launch (start us, length us, event | category | flops | bytes accessed | tf_op | source)
XLA Modules:
  0.0 366.0 jit_solution(3246682681318288068)
XLA Ops:
  8.2 0.8 select_reduce_fusion
  9.7 1.6 fusion.6
  11.3 20.5 %all-to-all-start = ((bf16[32,8,2048]{2,1,0:T(8,128)(2,1)}), bf16[32,8,2048]{2,1,0:T(8,128)(2,1)S(1)}, u32[]{:S(2)}, u32[]{:S(2)}) async-start(bf16[32,8,2048]{2,1,0:T(8,128)(2,1)} %fusion.6), calls=%async_computation | async-start | bytes 2097152 | tf_op jit(solution)/shard_map/all_to_all | solution.py:44
  31.8 1.5 fusion.7
  33.4 28.5 %all-to-all-done = bf16[32,8,2048]{2,1,0:T(8,128)(2,1)S(1)} async-done(((bf16[32,8,2048]{2,1,0:T(8,128)(2,1)}), bf16[32,8,2048]{2,1,0:T(8,128)(2,1)S(1)}, u32[]{:S(2)}, u32[]{:S(2)}) %all-to-all-start) | async-done | bytes 1048608 | tf_op jit(solution)/shard_map/all_to_all | solution.py:44
  61.9 6.7 %all-to-all-start.2 = ((bf16[32,8,2048]{2,1,0:T(8,128)(2,1)}), bf16[32,8,2048]{2,1,0:T(8,128)(2,1)}, u32[]{:S(2)}, u32[]{:S(2)}) async-start(bf16[32,8,2048]{2,1,0:T(8,128)(2,1)} %fusion.7), calls=%async_computation.3 | async-start | bytes 2097152 | tf_op jit(solution)/shard_map/all_to_all | solution.py:45
  68.7 40.8 %all_gather.9 = bf16[2,2048,96]{1,2,0:T(8,128)(2,1)S(1)} all-gather(bf16[2,512,96]{1,2,0:T(8,128)(2,1)S(1)} %copy-done.7), channel_id=1, replica_groups=mesh['dp'=4,'expert'=32,'tensor'=8] {'dp'}, dimensions={1}, use_global_device_ids=true | all-gather | bytes 983040 | tf_op jit(solution)/shard_map/all_gather | solution.py:39
  109.6 15.4 %all_gather.10 = bf16[2,2048,96]{1,2,0:T(8,128)(2,1)S(1)} all-gather(bf16[2,512,96]{1,2,0:T(8,128)(2,1)S(1)} %copy-done.8), channel_id=1, replica_groups=mesh['dp'=4,'expert'=32,'tensor'=8] {'dp'}, dimensions={1}, use_global_device_ids=true | all-gather | bytes 983040 | tf_op jit(solution)/shard_map/all_gather | solution.py:40
  125.0 15.7 %all_gather.11 = bf16[2,96,2048]{2,1,0:T(8,128)(2,1)} all-gather(bf16[2,96,512]{2,1,0:T(8,128)(2,1)S(1)} %copy-done.9), channel_id=1, replica_groups=mesh['dp'=4,'expert'=32,'tensor'=8] {'dp'}, dimensions={2}, use_global_device_ids=true | all-gather | bytes 983040 | tf_op jit(solution)/shard_map/all_gather | solution.py:41
  140.7 1.8 copy.18
  142.9 1.1 convolution_bitcast_fusion.5
  144.0 1.9 copy.20
  145.9 1.0 copy-done.1
  147.3 1.4 fusion.4
  149.2 1.4 fusion.5
  150.7 2.1 fusion.3
  152.9 1.3 fusion.2
  154.3 1.3 fusion.1
  155.7 37.4 %reduce-scatter.6.cloned.1.call-done = bf16[32,2,4,256]{3,0,2,1:T(8,128)(2,1)} async-done(((bf16[32,2,4,2048]{3,0,2,1:T(8,128)(2,1)}), bf16[32,2,4,256]{3,0,2,1:T(8,128)(2,1)}) %reduce-scatter.6.cloned.1.call-update) | async-done | bytes 131088 | tf_op jit(solution)/shard_map/reduce_scatter | solution.py:70
  193.0 1.7 copy.19
  194.7 17.8 %all-to-all-start.1 = ((bf16[32,2,4,256]{3,2,1,0:T(4,128)(2,1)}), bf16[32,2,4,256]{3,2,1,0:T(4,128)(2,1)S(1)}, u32[]{:S(2)}, u32[]{:S(2)}) async-start(bf16[32,2,4,256]{3,2,1,0:T(4,128)(2,1)} %copy.19), calls=%async_computation.2 | async-start | bytes 262144 | tf_op jit(solution)/shard_map/all_to_all | solution.py:78
  212.5 26.9 %reduce-scatter.8.cloned.1.call-done = bf16[32,2,4,256]{3,0,2,1:T(8,128)(2,1)} async-done(((bf16[32,2,4,2048]{3,0,2,1:T(8,128)(2,1)}), bf16[32,2,4,256]{3,0,2,1:T(8,128)(2,1)}) %reduce-scatter.8.cloned.1.call-update) | async-done | bytes 131088 | tf_op jit(solution)/shard_map/reduce_scatter | solution.py:73
  239.4 1.7 copy.21
  241.1 18.3 %all-to-all-start.3 = ((bf16[32,2,4,256]{3,2,1,0:T(4,128)(2,1)}), bf16[32,2,4,256]{3,2,1,0:T(4,128)(2,1)S(1)}, u32[]{:S(2)}, u32[]{:S(2)}) async-start(bf16[32,2,4,256]{3,2,1,0:T(4,128)(2,1)} %copy.21), calls=%async_computation.5 | async-start | bytes 262144 | tf_op jit(solution)/shard_map/all_to_all | solution.py:81
  259.4 22.8 %reduce-scatter.14.cloned.1.call-done = bf16[2,96,512]{2,1,0:T(8,128)(2,1)} async-done(((bf16[2,96,2048]{2,1,0:T(8,128)(2,1)}), bf16[2,96,512]{2,1,0:T(8,128)(2,1)}) %reduce-scatter.14.cloned.1.call-update) | async-done | bytes 196624 | tf_op jit(solution)/shard_map/reduce_scatter | solution.py:101
  282.2 1.7 convert_element_type.88
  283.9 34.3 %reduce-scatter.12.cloned.1.call-done = bf16[2,512,96]{1,2,0:T(8,128)(2,1)} async-done(((bf16[2,2048,96]{1,2,0:T(8,128)(2,1)}), bf16[2,512,96]{1,2,0:T(8,128)(2,1)}) %reduce-scatter.12.cloned.1.call-update) | async-done | bytes 196624 | tf_op jit(solution)/shard_map/reduce_scatter | solution.py:98
  318.3 1.7 convert_element_type.86
  320.0 36.0 %reduce-scatter.10.cloned.1.call-done = bf16[2,512,96]{1,2,0:T(8,128)(2,1)} async-done(((bf16[2,2048,96]{1,2,0:T(8,128)(2,1)}), bf16[2,512,96]{1,2,0:T(8,128)(2,1)}) %reduce-scatter.10.cloned.1.call-update) | async-done | bytes 196624 | tf_op jit(solution)/shard_map/reduce_scatter | solution.py:95
  355.9 1.7 convert_element_type.84
  357.7 0.9 convolution_convert_fusion.4
  358.6 0.8 convolution_convert_fusion.3
  (47 shorter events, 3.4 us)
Async XLA Ops:
  7.2 2.5 copy-start
  7.2 24.6 %copy-start.11 = (f32[128,8]{0,1:T(8,128)S(1)}, f32[128,8]{0,1:T(8,128)}, u32[]{:S(2)}) copy-start(f32[128,8]{0,1:T(8,128)} %param.9) | copy-start | bytes 12292
  7.2 24.6 %copy-start.5 = (bf16[128,2048]{1,0:T(8,128)(2,1)S(1)}, bf16[128,2048]{1,0:T(8,128)(2,1)}, u32[]{:S(2)}) copy-start(bf16[128,2048]{1,0:T(8,128)(2,1)} %param.8) | copy-start | bytes 1572868
  11.3 50.6 %all-to-all-start = ((bf16[32,8,2048]{2,1,0:T(8,128)(2,1)}), bf16[32,8,2048]{2,1,0:T(8,128)(2,1)S(1)}, u32[]{:S(2)}, u32[]{:S(2)}) async-start(bf16[32,8,2048]{2,1,0:T(8,128)(2,1)} %fusion.6), calls=%async_computation | async-start | bytes 2097152 | tf_op jit(solution)/shard_map/all_to_all | solution.py:44
  31.8 36.9 %copy-start.7 = (bf16[2,512,96]{1,2,0:T(8,128)(2,1)S(1)}, bf16[2,512,96]{1,2,0:T(8,128)(2,1)}, u32[]{:S(2)}) copy-start(bf16[2,512,96]{1,2,0:T(8,128)(2,1)} %param.11) | copy-start | bytes 589828
  31.8 77.7 %copy-start.8 = (bf16[2,512,96]{1,2,0:T(8,128)(2,1)S(1)}, bf16[2,512,96]{1,2,0:T(8,128)(2,1)}, u32[]{:S(2)}) copy-start(bf16[2,512,96]{1,2,0:T(8,128)(2,1)} %param.12) | copy-start | bytes 589828
  33.4 91.6 %copy-start.9 = (bf16[2,96,512]{2,1,0:T(8,128)(2,1)S(1)}, bf16[2,96,512]{2,1,0:T(8,128)(2,1)}, u32[]{:S(2)}) copy-start(bf16[2,96,512]{2,1,0:T(8,128)(2,1)} %param.13) | copy-start | bytes 589828
  61.9 63.1 %copy-start.3 = (bf16[32,8,2048]{2,1,0:T(8,128)(2,1)}, bf16[32,8,2048]{2,1,0:T(8,128)(2,1)S(1)}, u32[]{:S(2)}) copy-start(bf16[32,8,2048]{2,1,0:T(8,128)(2,1)S(1)} %all-to-all-done) | copy-start | bytes 3145732
  61.9 82.1 %all-to-all-start.2 = ((bf16[32,8,2048]{2,1,0:T(8,128)(2,1)}), bf16[32,8,2048]{2,1,0:T(8,128)(2,1)}, u32[]{:S(2)}, u32[]{:S(2)}) async-start(bf16[32,8,2048]{2,1,0:T(8,128)(2,1)} %fusion.7), calls=%async_computation.3 | async-start | bytes 2097152 | tf_op jit(solution)/shard_map/all_to_all | solution.py:45
  68.7 124.4 %reduce-scatter.6.cloned.1.call-start = ((), (), s32[]{:S(2)}) async-start(), calls=%async_computation.9 | async-start | bytes 1179648 | tf_op jit(solution)/shard_map/reduce_scatter | solution.py:70
  144.0 2.9 copy-start.4
  144.0 2.9 copy-start.10
  145.9 1.0 copy-start.1
  147.3 1.9 copy-start.6
  148.7 90.7 %reduce-scatter.8.cloned.1.call-start = ((), (), s32[]{:S(2)}) async-start(), calls=%async_computation.10 | async-start | bytes 1179648 | tf_op jit(solution)/shard_map/reduce_scatter | solution.py:73
  149.2 1.5 copy-start.2
  150.7 131.6 %reduce-scatter.14.cloned.1.call-start = ((), (), s32[]{:S(2)}) async-start(), calls=%async_computation.13 | async-start | bytes 983040 | tf_op jit(solution)/shard_map/reduce_scatter | solution.py:101
  152.9 165.4 %reduce-scatter.12.cloned.1.call-start = ((), (), s32[]{:S(2)}) async-start(), calls=%async_computation.12 | async-start | bytes 983040 | tf_op jit(solution)/shard_map/reduce_scatter | solution.py:98
  154.3 201.6 %reduce-scatter.10.cloned.1.call-start = ((), (), s32[]{:S(2)}) async-start(), calls=%async_computation.11 | async-start | bytes 983040 | tf_op jit(solution)/shard_map/reduce_scatter | solution.py:95
  194.7 46.4 %all-to-all-start.1 = ((bf16[32,2,4,256]{3,2,1,0:T(4,128)(2,1)}), bf16[32,2,4,256]{3,2,1,0:T(4,128)(2,1)S(1)}, u32[]{:S(2)}, u32[]{:S(2)}) async-start(bf16[32,2,4,256]{3,2,1,0:T(4,128)(2,1)} %copy.19), calls=%async_computation.2 | async-start | bytes 262144 | tf_op jit(solution)/shard_map/all_to_all | solution.py:78
  241.1 117.5 %all-to-all-start.3 = ((bf16[32,2,4,256]{3,2,1,0:T(4,128)(2,1)}), bf16[32,2,4,256]{3,2,1,0:T(4,128)(2,1)S(1)}, u32[]{:S(2)}, u32[]{:S(2)}) async-start(bf16[32,2,4,256]{3,2,1,0:T(4,128)(2,1)} %copy.21), calls=%async_computation.5 | async-start | bytes 262144 | tf_op jit(solution)/shard_map/all_to_all | solution.py:81
Sparse Core Ops, SparseCore 0:
  148.8 44.1 reduce-scatter.5
  196.4 42.9 reduce-scatter.7
  242.9 39.3 reduce-scatter.13
  285.5 32.6 reduce-scatter.11
  321.5 34.3 reduce-scatter.9
where the time goes:
time: 367 us; the launch traced here: 366 us
  waiting for transfers between devices  186 us (51%)
  blocking collectives  71.9 us (20%)
  starting transfers between devices  63.6 us (17%)
  matrix products  14.8 us (4%)
  between operations  14 us (4%)
  local copies, waits for them, and re-layouts  8.11 us (2%)
  other arithmetic  7.65 us (2%)
    all_gather x1, blocking collectives, on_device(): lax.all_gather(w_gate, 'dp', axis=1, tiled=True)  40.8 us
    reduce_scatter x1, waiting for transfers between devices, on_device(): lax.psum_scatter(part_out.astype(jnp.bfloat16), 'tensor', scatter_dimensi...  37.4 us
    reduce_scatter x1, waiting for transfers between devices, on_device(): lax.psum_scatter(term_gate.astype(jnp.bfloat16), 'dp', scatter_dimension=...  36 us
    reduce_scatter x1, waiting for transfers between devices, on_device(): lax.psum_scatter(term_up.astype(jnp.bfloat16), 'dp', scatter_dimension=1,...  34.3 us
    all_to_all x1, waiting for transfers between devices, on_device(): lax.all_to_all(send_x, 'expert', split_axis=0, concat_axis=0, tiled=True)  28.5 us
    reduce_scatter x1, waiting for transfers between devices, on_device(): lax.psum_scatter(part_in.astype(jnp.bfloat16), 'tensor', scatter_dimensio...  26.9 us
    reduce_scatter x1, waiting for transfers between devices, on_device(): lax.psum_scatter(term_down.astype(jnp.bfloat16), 'dp', scatter_dimension=...  22.8 us
    all_to_all x1, starting transfers between devices, on_device(): lax.all_to_all(send_x, 'expert', split_axis=0, concat_axis=0, tiled=True)  20.5 us
  transfers between devices with their start and end apart: 9, of which 6 were waited for; matrix products, arithmetic and copies ran while one was open for 6% of the time, Pallas kernels for 0%

commit v1 on v0

v1 whole, which is shorter than its diff:
```python
import functools

import jax
import jax.numpy as jnp
from jax import lax
from jax.experimental import pallas as pl
from jax.experimental.pallas import tpu as pltpu
from jax.sharding import PartitionSpec as P

MESH = pl.DeviceIdType.MESH
F32 = jnp.float32
BF16 = jnp.bfloat16
CAP = 4
LANES = 128
NT = (((1,), (1,)), ((), ()))
TN = (((0,), (0,)), ((), ()))


def dot(a, b, dims=(((1,), (0,)), ((), ()))):
    return lax.dot_general(a, b, dims, preferred_element_type=F32)


def kernel(
    cfg,
    tok, cot, sco, rou, wg, wu, wd,
    out, gtk, gg, gu, gd,
    sb, xb, wgu, wdn, pf, ps, pr, hb, ga2, hid2, part, ss, rv, fin, rb, slots,
    dsp_s, dsp_r, ag_s, ag_r, b_s, b_r, c_s, c_r, rs_s, rs_r, rt_s, rt_r,
):
    ZL, ZH, X, C, Y = cfg
    J = ZL * ZH * C
    R = J * 8
    GR = ZH * C * 8
    HALF = R // 2
    S = Y // 2
    HN = Y // ZL
    NE = ZH * X * C
    T = tok.shape[0]
    DS = wg.shape[1]
    FS = wg.shape[2]
    CW = out.shape[1]

    d = lax.axis_index("dp")
    e = lax.axis_index("expert")
    t = lax.axis_index("tensor")
    zh = e // (X * C)
    x = (e // C) % X
    c = e % C
    hop = (Y // 2) * zh + (Y // 4) * c
    jme = d * (ZH * C) + zh * C + c
    right = (d, e, (t + 1) % Y)
    left = (d, e, (t + Y - 1) % Y)

    def peer(j):
        zl_p = j // (ZH * C)
        zh_p = (j // C) % ZH
        c_p = j % C
        x_p = (t + 8 * Y - x - hop - (Y // 2) * zh_p - (Y // 4) * c_p) % X
        e_p = zh_p * (X * C) + x_p * C + c_p
        return zl_p, e_p

    def same(zl_p, e_p, t_p):
        return jnp.logical_and(jnp.logical_and(zl_p == d, e_p == e), t_p == t)

    barrier = pltpu.get_barrier_semaphore()

    def greet(zl_p, e_p, t_p):
        me = same(zl_p, e_p, t_p)

        @pl.when(jnp.logical_not(me))
        def _():
            pl.semaphore_signal(barrier, inc=1, device_id=(zl_p, e_p, t_p), device_id_type=MESH)

        return jnp.where(me, 0, 1)

    def greet_dispatch(j, n):
        zl_p, e_p = peer(j)
        return n + greet(zl_p, e_p, t)

    def greet_return(i, n):
        zl_p = t // HN
        hop_p = (Y // 2) * (i // (X * C)) + (Y // 4) * (i % C)
        return n + greet(zl_p, i, (x + hop + (i // C) % X + hop_p) % Y)

    count = lax.fori_loop(0, J, greet_dispatch, jnp.int32(0))
    count = lax.fori_loop(0, NE, greet_return, count)
    for dev in (right, left):
        pl.semaphore_signal(barrier, inc=1, device_id=dev, device_id_type=MESH)
    for o in range(1, ZL):
        pl.semaphore_signal(barrier, inc=1, device_id=((d + o) % ZL, e, t), device_id_type=MESH)

    sub = lax.broadcasted_iota(jnp.int32, (T, T), 0)
    lan = lax.broadcasted_iota(jnp.int32, (T, T), 1)
    rcol = rou[...]
    rrow = jnp.sum(jnp.where(sub == lan, rcol, 0), axis=0, keepdims=True)
    place = jnp.sum(jnp.where((rcol == rrow) & (lan < sub), 1, 0), axis=1, keepdims=True)
    scol = rcol * CAP + place
    slots[...] = scol
    srow = jnp.sum(jnp.where(sub == lan, scol, 0), axis=0, keepdims=True)
    row = lax.broadcasted_iota(jnp.int32, (R, T), 0)
    jv = row // 8
    zh_v = (jv // C) % ZH
    c_v = jv % C
    x_v = (t + 8 * Y - x - hop - (Y // 2) * zh_v - (Y // 4) * c_v) % X
    want = (zh_v * (X * C) + x_v * C + c_v) * 8 + row % 8
    pick = jnp.where(want == srow, 1.0, 0.0).astype(BF16)
    scores = sco[...]
    mix = scores[:, 0:1] / jnp.sum(scores, axis=1, keepdims=True)
    for g in range(ZL):
        cols = slice(g * DS, (g + 1) * DS)
        rows = slice(g * GR, (g + 1) * GR)
        sb[rows, 0:DS] = dot(pick[rows], tok[:, cols]).astype(BF16)
        dg = (mix * cot[:, cols].astype(F32)).astype(BF16)
        sb[rows, DS : 2 * DS] = dot(pick[rows], dg).astype(BF16)

    pl.semaphore_wait(barrier, count + 2 + ZL - 1)

    def dsp_copy(j, zl_p, e_p, slot):
        return pltpu.make_async_remote_copy(
            src_ref=sb.at[pl.ds(pl.multiple_of(j * 8, 8), 8), :],
            dst_ref=xb.at[0, pl.ds(pl.multiple_of(slot * 8, 8), 8), :],
            send_sem=dsp_s.at[j],
            recv_sem=dsp_r.at[slot],
            device_id=(zl_p, e_p, t),
            device_id_type=MESH,
        )

    def dsp_local(j):
        rows = pl.ds(pl.multiple_of(j * 8, 8), 8)
        return pltpu.make_async_copy(sb.at[rows, :], xb.at[0, rows, :], dsp_r.at[j])

    def dsp_start(j, carry):
        zl_p, e_p = peer(j)
        me = same(zl_p, e_p, t)

        @pl.when(me)
        def _():
            dsp_local(j).start()

        @pl.when(jnp.logical_not(me))
        def _():
            dsp_copy(j, zl_p, e_p, jme).start()

        return carry

    lax.fori_loop(0, J, dsp_start, 0)

    wgu[...] = jnp.zeros_like(wgu)
    wdn[...] = jnp.zeros_like(wdn)
    for n in range(2):
        wgu[:, n * LANES : n * LANES + FS] = wg[n]
        wgu[:, (2 + n) * LANES : (2 + n) * LANES + FS] = wu[n]
        wdn[n * LANES : n * LANES + FS, :] = wd[n]
    first = lax.broadcasted_iota(jnp.int32, (R, LANES), 0) % 8 < CAP
    m0 = jnp.where(first, 1.0, 0.0).astype(BF16)
    m1 = jnp.where(first, 0.0, 1.0).astype(BF16)

    def dsp_wait(j, carry):
        dsp_local(j).wait()
        return carry

    lax.fori_loop(0, J, dsp_wait, 0)

    def ag_copy(way, s, hf):
        src = (-s) % Y if way == 0 else s
        dst = (-s - 1) % Y if way == 0 else s + 1
        rows = pl.ds(hf * HALF, HALF)
        return pltpu.make_async_remote_copy(
            src_ref=xb.at[src, rows, :],
            dst_ref=xb.at[dst, rows, :],
            send_sem=ag_s.at[way, s, hf],
            recv_sem=ag_r.at[way, s, hf],
            device_id=right if way == 0 else left,
            device_id_type=MESH,
        )

    def ag_live(way, s, hf):
        return s < S - 1 or hf == way

    def ag_start(s, way, hf):
        if s < S and ag_live(way, s, hf):
            ag_copy(way, s, hf).start()

    def b_copy(k, o):
        g = (d + o) % ZL
        return pltpu.make_async_remote_copy(
            src_ref=ps.at[k, g],
            dst_ref=pr.at[k, o - 1],
            send_sem=b_s.at[k, o - 1],
            recv_sem=b_r.at[k, o - 1],
            device_id=(g, e, t),
            device_id_type=MESH,
        )

    def c_copy(k, o):
        return pltpu.make_async_remote_copy(
            src_ref=hb.at[k, d],
            dst_ref=hb.at[k, d],
            send_sem=c_s.at[k, o - 1],
            recv_sem=c_r.at[k, o - 1],
            device_id=((d + o) % ZL, e, t),
            device_id_type=MESH,
        )

    def partial(k):
        xg = dot(xb[k, :, 0:DS], wgu[...])
        bk = dot(xb[k, :, DS : 2 * DS], wdn[...], NT)
        sel = [
            jnp.where(first, xg[:, 0:LANES], xg[:, LANES : 2 * LANES]),
            jnp.where(first, xg[:, 2 * LANES : 3 * LANES], xg[:, 3 * LANES : 4 * LANES]),
            jnp.where(first, bk[:, 0:LANES], bk[:, LANES : 2 * LANES]),
        ]
        for n in range(3):
            cols = slice(n * LANES, (n + 1) * LANES)
            val = sel[n].reshape(ZL, GR, LANES)
            pf[k, :, :, cols] = val
            ps[k, :, :, cols] = val.astype(BF16)
        for o in range(1, ZL):
            b_copy(k, o).start()

    def activate(k):
        for o in range(1, ZL):
            b_copy(k, o).wait_recv()
        acts = pf[k, d]
        for o in range(1, ZL):
            acts = acts + pr[k, o - 1].astype(F32)
        gate = acts[:, 0:LANES]
        up = acts[:, LANES : 2 * LANES]
        back = acts[:, 2 * LANES : 3 * LANES]
        sig = jax.nn.sigmoid(gate)
        silu = gate * sig
        hb[k, d, :, 0:LANES] = (silu * up).astype(BF16)
        hb[k, d, :, LANES : 2 * LANES] = (back * up * sig * (1.0 + gate * (1.0 - sig))).astype(BF16)
        hb[k, d, :, 2 * LANES : 3 * LANES] = (back * silu).astype(BF16)
        for o in range(1, ZL):
            c_copy(k, o).start()

    def c_wait(k):
        for o in range(1, ZL):
            g = (d + ZL - o) % ZL
            pltpu.make_async_remote_copy(
                src_ref=hb.at[k, g],
                dst_ref=hb.at[k, g],
                send_sem=c_s.at[k, o - 1],
                recv_sem=c_r.at[k, o - 1],
                device_id=((d + o) % ZL, e, t),
                device_id_type=MESH,
            ).wait_recv()

    def finish(k):
        c_wait(k)
        acts = hb[k].reshape(R, 3 * LANES)
        hid = acts[:, 0:LANES]
        hid2[k, :, 0:LANES] = hid * m0
        hid2[k, :, LANES : 2 * LANES] = hid * m1
        for n in range(2):
            ga = acts[:, (1 + n) * LANES : (2 + n) * LANES]
            ga2[k, :, 2 * n * LANES : (2 * n + 1) * LANES] = ga * m0
            ga2[k, :, (2 * n + 1) * LANES : (2 * n + 2) * LANES] = ga * m1
        part[k, :, 0:DS] = dot(hid2[k], wdn[...])
        part[k, :, DS : 2 * DS] = dot(ga2[k], wgu[...], NT)

    for hf in range(2):
        for way in range(2):
            ag_start(0, way, hf)
    partial(0)
    late = [0]
    for s in range(S):
        for hf in range(2):
            for way in range(2):
                if ag_live(way, s, hf):
                    ag_copy(way, s, hf).wait_recv()
                    ag_start(s + 1, way, hf)
        fresh = sorted({(-s - 1) % Y, s + 1})
        for k in fresh:
            partial(k)
        for k in late:
            activate(k)
        late = fresh
    for k in late:
        activate(k)

    def rs_copy(way, s, ch):
        cols = pl.ds(ch * DS, DS)
        return pltpu.make_async_remote_copy(
            src_ref=ss.at[way, s, :, cols],
            dst_ref=rv.at[way, s, :, cols],
            send_sem=rs_s.at[way, s, ch],
            recv_sem=rs_r.at[way, s, ch],
            device_id=right if way == 0 else left,
            device_id_type=MESH,
        )

    def rs_live(way, s, ch):
        return s > 0 or ch == way

    def rs_send(way, s, ch):
        if not rs_live(way, s, ch):
            return
        k = S - s if way == 0 else (s - S) % Y
        cols = slice(ch * DS, (ch + 1) * DS)
        val = part[k, :, cols]
        if s > 0 and rs_live(way, s - 1, ch):
            rs_copy(way, s - 1, ch).wait_recv()
            val = val + rv[way, s - 1, :, cols].astype(F32)
        ss[way, s, :, cols] = val.astype(BF16)
        rs_copy(way, s, ch).start()

    def grads():
        xs = xb[:, :, 0:DS].reshape(Y * R, DS)
        ggu = dot(xs, ga2[...].reshape(Y * R, 4 * LANES), TN)
        for n in range(2):
            gg[n] = ggu[:, n * LANES : n * LANES + FS]
            gu[n] = ggu[:, (2 + n) * LANES : (2 + n) * LANES + FS]
        ds_ = xb[:, :, DS : 2 * DS].reshape(Y * R, DS)
        gdn = dot(hid2[...].reshape(Y * R, 2 * LANES), ds_, TN)
        for n in range(2):
            gd[n] = gdn[n * LANES : n * LANES + FS]

    finish(S)
    rs_send(0, 0, 0)
    rs_send(1, 0, 1)
    for k in range(S - 1, 0, -1):
        finish(k)
        finish(Y - k)
    finish(0)
    for s in range(1, S):
        order = [(0, 0), (1, 1), (0, 1), (1, 0)] if s > 1 else [(0, 1), (1, 0), (0, 0), (1, 1)]
        for way, ch in order:
            rs_send(way, s, ch)
        if s == 1:
            grads()
    if S == 1:
        grads()

    for ch in range(2):
        cols = slice(ch * DS, (ch + 1) * DS)
        val = part[0, :, cols]
        for way in range(2):
            if rs_live(way, S - 1, ch):
                rs_copy(way, S - 1, ch).wait_recv()
                val = val + rv[way, S - 1, :, cols].astype(F32)
        val = val.astype(BF16)
        for h in range(HN):
            fin[h, :, ch * CW : (ch + 1) * CW] = val[:, h * CW : (h + 1) * CW]

    def rt_copy(i, zl_p, e_p, t_p):
        j = i // HN
        return pltpu.make_async_remote_copy(
            src_ref=fin.at[i % HN, pl.ds(pl.multiple_of(j * 8, 8), 8), :],
            dst_ref=rb.at[pl.ds(pl.multiple_of(e * 8, 8), 8), :],
            send_sem=rt_s.at[i],
            recv_sem=rt_r.at[e],
            device_id=(zl_p, e_p, t_p),
            device_id_type=MESH,
        )

    def rt_local(h, j, slot):
        return pltpu.make_async_copy(
            fin.at[h, pl.ds(pl.multiple_of(j * 8, 8), 8), :],
            rb.at[pl.ds(pl.multiple_of(slot * 8, 8), 8), :],
            rt_r.at[slot],
        )

    def rt_start(i, carry):
        zl_p, e_p = peer(i // HN)
        t_p = HN * d + i % HN
        me = same(zl_p, e_p, t_p)

        @pl.when(me)
        def _():
            rt_local(i % HN, i // HN, e).start()

        @pl.when(jnp.logical_not(me))
        def _():
            rt_copy(i, zl_p, e_p, t_p).start()

        return carry

    lax.fori_loop(0, J * HN, rt_start, 0)

    def rt_wait(i, carry):
        rt_local(0, 0, i).wait()
        return carry

    lax.fori_loop(0, NE, rt_wait, 0)

    slot_lane = lax.broadcasted_iota(jnp.int32, (T, NE * 8), 1)
    take = jnp.where(slots[...] == slot_lane, 1.0, 0.0).astype(BF16)
    res = dot(take, rb[...])
    scores = sco[...]
    mix = scores[:, 0:1] / jnp.sum(scores, axis=1, keepdims=True)
    out[...] = (mix * res[:, 0:CW]).astype(BF16)
    gtk[...] = res[:, CW : 2 * CW].astype(BF16)

    def dsp_done(j, carry):
        zl_p, e_p = peer(j)

        @pl.when(jnp.logical_not(same(zl_p, e_p, t)))
        def _():
            dsp_copy(j, zl_p, e_p, jme).wait_send()

        return carry

    lax.fori_loop(0, J, dsp_done, 0)
    for s in range(S):
        for way in range(2):
            for ch in range(2):
                if ag_live(way, s, ch):
                    ag_copy(way, s, ch).wait_send()
                if rs_live(way, s, ch):
                    rs_copy(way, s, ch).wait_send()
    for k in range(Y):
        for o in range(1, ZL):
            b_copy(k, o).wait_send()
            c_copy(k, o).wait_send()

    def rt_done(i, carry):
        zl_p, e_p = peer(i // HN)
        t_p = HN * d + i % HN

        @pl.when(jnp.logical_not(same(zl_p, e_p, t_p)))
        def _():
            rt_copy(i, zl_p, e_p, t_p).wait_send()

        return carry

    lax.fori_loop(0, J * HN, rt_done, 0)


def on_device(cfg, tokens, cotangent, scores, routes, w_gate, w_up, w_down):
    ZL, ZH, X, C, Y = cfg
    J = ZL * ZH * C
    R = J * 8
    GR = ZH * C * 8
    S = Y // 2
    HN = Y // ZL
    NE = ZH * X * C
    T, D = tokens.shape
    _, DS, FS = w_gate.shape
    CW = D // Y
    L3 = 3 * LANES
    vm = pl.BlockSpec(memory_space=pltpu.VMEM)
    dma = pltpu.SemaphoreType.DMA
    return pl.pallas_call(
        functools.partial(kernel, cfg),
        out_shape=(
            jax.ShapeDtypeStruct((T, CW), BF16),
            jax.ShapeDtypeStruct((T, CW), BF16),
            jax.ShapeDtypeStruct(w_gate.shape, F32),
            jax.ShapeDtypeStruct(w_up.shape, F32),
            jax.ShapeDtypeStruct(w_down.shape, F32),
        ),
        in_specs=[vm] * 7,
        out_specs=(vm,) * 5,
        scratch_shapes=[
            pltpu.VMEM((R, 2 * DS), BF16),
            pltpu.VMEM((Y, R, 2 * DS), BF16),
            pltpu.VMEM((DS, 4 * LANES), BF16),
            pltpu.VMEM((2 * LANES, DS), BF16),
            pltpu.VMEM((Y, ZL, GR, L3), F32),
            pltpu.VMEM((Y, ZL, GR, L3), BF16),
            pltpu.VMEM((Y, ZL - 1, GR, L3), BF16),
            pltpu.VMEM((Y, ZL, GR, L3), BF16),
            pltpu.VMEM((Y, R, 4 * LANES), BF16),
            pltpu.VMEM((Y, R, 2 * LANES), BF16),
            pltpu.VMEM((Y, R, 2 * DS), F32),
            pltpu.VMEM((2, S, R, 2 * DS), BF16),
            pltpu.VMEM((2, S, R, 2 * DS), BF16),
            pltpu.VMEM((HN, R, 2 * CW), BF16),
            pltpu.VMEM((NE * 8, 2 * CW), BF16),
            pltpu.VMEM((T, 1), jnp.int32),
            dma((J,)),
            dma((J,)),
            dma((2, S, 2)),
            dma((2, S, 2)),
            dma((Y, ZL - 1)),
            dma((Y, ZL - 1)),
            dma((Y, ZL - 1)),
            dma((Y, ZL - 1)),
            dma((2, S, 2)),
            dma((2, S, 2)),
            dma((J * HN,)),
            dma((NE,)),
        ],
        compiler_params=pltpu.CompilerParams(
            collective_id=0, has_side_effects=True, vmem_limit_bytes=60 * 1024 * 1024
        ),
        name="expert_layer",
    )(tokens, cotangent, scores, routes, w_gate, w_up, w_down)


def solution(mesh, cfg=(4, 2, 8, 2, 8)):
    in_specs = (
        P(("dp", "expert"), None),
        P(("dp", "expert"), None),
        P(("dp", "expert"), None),
        P(("dp", "expert"), None),
        P("expert", "dp", "tensor"),
        P("expert", "dp", "tensor"),
        P("expert", "tensor", "dp"),
    )
    out_specs = (
        P(("dp", "expert"), "tensor"),
        P(("dp", "expert"), "tensor"),
        P("expert", "dp", "tensor"),
        P("expert", "dp", "tensor"),
        P("expert", "tensor", "dp"),
    )
    return jax.shard_map(
        functools.partial(on_device, cfg),
        mesh=mesh,
        in_specs=in_specs,
        out_specs=out_specs,
        check_vma=False,
    )
```

time: 367 us -> 142 us (0.39)
  the two profiles are of different devices: /device:TPU:1 before, /device:TPU:7 now
where the time goes in v1:
time: 142 us
  Pallas kernels  131 us (92%)
  local copies, waits for them, and re-layouts  10 us (7%)
    pallas_call x1, Pallas kernels, on_device(): pl.pallas_call(functools.partial(kernel, cfg), out_shape=(jax.ShapeDtypeS...  131 us
    unnamed x19, local copies, waits for them, and re-layouts  7.06 us
    pallas_call x2, local copies, waits for them, and re-layouts, on_device(): pl.pallas_call(functools.partial(kernel, cfg), out_shape=(jax.ShapeDtypeS...  2.98 us

profile of v1, /device:TPU:7, one launch (start us, length us, event | category | flops | bytes accessed | tf_op | source)
XLA Modules:
  0.0 142.2 jit_solution(6482205157969773266)
XLA Ops:
  0.6 0.0 copy-start.5
  0.6 1.4 copy.12.sco
  2.1 0.0 copy-done.5
  2.1 0.7 copy.13.rou
  2.8 0.0 copy-start.2
  2.8 1.8 %copy.14.wg = bf16[2,512,96]{2,1,0:T(8,128)(2,1)} copy(bf16[2,512,96]{1,2,0:T(8,128)(2,1)} %param.11) | data formatting | bytes 393216 | tf_op args[4]
  4.6 0.0 copy-done.2
  4.6 0.8 copy.15.wu
  5.5 131.5 %expert_layer.1 = (bf16[128,256]{1,0:T(8,128)(2,1)}, bf16[128,256]{1,0:T(8,128)(2,1)}, f32[2,512,96]{2,1,0:T(8,128)}, f32[2,512,96]{2,1,0:T(8,128)}, f32[2,96,512]{2,1,0:T(8,128)}) custom-call(bf16[128,2048]{1,0:T(8,128)(2,1)} %tok.1, bf16[128,2048]{1,0:T(8,128)(2,1)} %cot.1, f32[128,8]{1,0:T(8,128)} %copy.12.sco, s32[128,1]{1,0:T(8,128)} %copy.13.rou, ...), custom_call_target="tpu_custom_call" | custom-call | tf_op jit(solution)/shard_map/expert_layer/pallas_call | solution.py:445
  136.9 0.0 copy-start
  136.9 2.0 %copy.16 = f32[2,512,96]{1,2,0:T(8,128)} copy(f32[2,512,96]{2,1,0:T(8,128)} %get-tuple-element.7) | data formatting | bytes 786432 | tf_op jit(solution)/shard_map/expert_layer/pallas_call | solution.py:445
  139.0 0.0 copy-done
  139.0 0.0 copy-start.4
  139.0 0.0 copy-start.1
  139.0 0.9 copy.17
  139.9 0.0 copy-done.4
  139.9 0.0 copy-start.3
  139.9 0.6 copy.21
  140.6 0.2 copy-done.3
  140.8 0.6 copy.22
  141.4 0.0 copy-done.1
  141.4 0.7 copy.23
Async XLA Ops:
  0.6 1.4 %copy-start.5 = (s32[128,1]{0,1:T(1,128)S(1)}, s32[128,1]{0,1:T(1,128)}, u32[]{:S(2)}) copy-start(s32[128,1]{0,1:T(1,128)} %param.10) | copy-start | bytes 1540
  2.8 1.8 %copy-start.2 = (bf16[2,512,96]{1,2,0:T(8,128)(2,1)S(1)}, bf16[2,512,96]{1,2,0:T(8,128)(2,1)}, u32[]{:S(2)}) copy-start(bf16[2,512,96]{1,2,0:T(8,128)(2,1)} %param.12) | copy-start | bytes 589828
  136.9 2.0 %copy-start = (f32[2,512,96]{2,1,0:T(8,128)S(1)}, f32[2,512,96]{2,1,0:T(8,128)}, u32[]{:S(2)}) copy-start(f32[2,512,96]{2,1,0:T(8,128)} %get-tuple-element.8) | copy-start | bytes 1179652
  139.0 0.9 copy-start.4
  139.0 2.4 %copy-start.1 = (f32[2,96,512]{2,1,0:T(8,128)S(1)}, f32[2,96,512]{2,1,0:T(8,128)}, u32[]{:S(2)}) copy-start(f32[2,96,512]{2,1,0:T(8,128)} %get-tuple-element.19) | copy-start | bytes 1179652
  139.9 0.9 copy-start.3
